TPU v7x, 512 devices: a whole 4x8x8 slice. The times are simulated.
512 devices in a mesh: row: 16 (over x_lo, z), col: 32 (over y, x_hi, core).
Axes of the slice: x: 4 (x_hi: 2, x_lo: 2; x = x_hi * 2 + x_lo), y: 8, z: 8, core: 2. Of those that a mesh axis runs over, the one named last changes fastest.
Arguments:
- protocols: float32 [20, 65536], P(None, ('row', 'col')), may hold values from -6 to 6
- w_in: float32 [20, 256], replicated, may hold values from -1.25 to 1.25
- b_in: float32 [256], replicated, may hold values from -3 to 3
- w_out: float32 [256, 64], replicated, may hold values from -0.21875 to 0.21875
- solved: float32 [32, 65536], P(None, ('row', 'col')), may hold values from -0.5 to 0.5
- probes: float32 [32, 65536], P(None, ('row', 'col')), may hold values from -6 to 6
- window_blocks: int32 [16], replicated, may hold values from 0 to 31
Outputs:
- col_grad: float32 [64, 65536], P(None, ('row', 'col'))
- grad_in: float32 [20, 256], replicated
- grad_bias: float32 [256], replicated
- grad_out: float32 [256, 64], replicated
Inputs may be any that keep to these rules, and one draw needn't show every extreme that they name: Window block r is the 128 protocols held at index r of row and index window_blocks[r] of col.
All inputs are finite; a program needn't handle non-finite values.
Results may differ from a plain program's by a relative error of at most 0.0003.
Values sent between devices are 32-bit elements; how exact they have to be, the bound alone decides.
A program may use at most 64 MiB of HBM per device.

v0:
```python
import jax
import jax.numpy as jnp
from jax import lax
from jax.sharding import PartitionSpec as P

HIGHEST = lax.Precision.HIGHEST


def spread(value, axis, source):
    kept = jnp.where(lax.axis_index(axis) == source, value, 0).astype(value.dtype)
    return lax.psum(kept, axis)


def tile_pass(first_feat, first_vec, second_feat, second_vec):
    first_norm = jnp.sum(first_feat * first_feat, 0)
    second_norm = jnp.sum(second_feat * second_feat, 0)
    cross = jnp.einsum("fi,fj->ij", first_feat, second_feat, precision=HIGHEST)
    kern = jnp.exp(-0.5 * (first_norm[:, None] + second_norm[None, :] - 2.0 * cross))
    weigh = jnp.einsum("qi,qj->ij", first_vec, second_vec, precision=HIGHEST) * kern
    first_grad = (
        jnp.einsum("fj,ij->fi", second_feat, weigh, precision=HIGHEST)
        - first_feat * jnp.sum(weigh, 1)[None, :]
    )
    second_grad = (
        jnp.einsum("fi,ij->fj", first_feat, weigh, precision=HIGHEST)
        - second_feat * jnp.sum(weigh, 0)[None, :]
    )
    return (first_grad, second_grad)


def blocked(first_feat, first_vec, second_feat, second_vec):
    width = second_feat.shape[1]
    block_width = 1024
    count = width // block_width
    split_feat = second_feat.reshape(second_feat.shape[0], count, block_width).transpose(1, 0, 2)
    split_vec = second_vec.reshape(second_vec.shape[0], count, block_width).transpose(1, 0, 2)

    def partial_pass(running, pair):
        first_part, second_part = tile_pass(first_feat, first_vec, pair[0], pair[1])
        return (running + first_part, second_part)

    first_grad, second_parts = lax.scan(
        partial_pass, jnp.zeros_like(first_feat), (split_feat, split_vec)
    )
    return (first_grad, second_parts.transpose(1, 0, 2).reshape(second_feat.shape[0], width))


def hidden_of(w_in, b_in, inputs):
    return jnp.tanh(jnp.einsum("ph,pn->hn", w_in, inputs, precision=HIGHEST) + b_in[:, None])


def backprop(w_out, inputs, hidden, grads):
    grad_out = jnp.einsum("hn,fn->hf", hidden, grads, precision=HIGHEST)
    grad_hidden = jnp.einsum("hf,fn->hn", w_out, grads, precision=HIGHEST)
    grad_pre = grad_hidden * (1.0 - hidden * hidden)
    grad_in = jnp.einsum("pn,hn->ph", inputs, grad_pre, precision=HIGHEST)
    return (grad_in, jnp.sum(grad_pre, 1), grad_out)


def window_total(partial_grad):
    return lax.psum(partial_grad, "col")


def per_device(protocols, w_in, b_in, w_out, solved, probes, window_blocks):
    hidden = hidden_of(w_in, b_in, protocols)
    features = jnp.einsum("hf,hn->fn", w_out, hidden, precision=HIGHEST)
    owner_col = window_blocks[lax.axis_index("row")]
    is_owner = lax.axis_index("col") == owner_col
    window = (spread(features, "col", owner_col), spread(solved, "col", owner_col))
    win_part, col_part = blocked(
        window[0],
        window[1],
        lax.all_gather(features, "row", axis=1, tiled=True),
        lax.all_gather(probes, "row", axis=1, tiled=True),
    )
    col_grad = lax.psum_scatter(col_part, "row", scatter_dimension=1, tiled=True)
    summed = window_total(win_part)
    own_total = col_grad + jnp.where(is_owner, summed, jnp.zeros_like(summed))
    terms = backprop(w_out, protocols, hidden, own_total)
    grad_in, grad_bias, grad_out = lax.psum((terms[0], terms[1], terms[2]), ("row", "col"))
    return (col_grad, grad_in, grad_bias, grad_out)


def solution(mesh):
    in_specs = (
        P(None, ("row", "col")),
        P(),
        P(),
        P(),
        P(None, ("row", "col")),
        P(None, ("row", "col")),
        P(),
    )
    out_specs = (P(None, ("row", "col")), P(), P(), P())
    return jax.shard_map(
        per_device, mesh=mesh, in_specs=in_specs, out_specs=out_specs, check_vma=False
    )
```

profile of v0, /device:TPU:1, one launch (start us, length us, event | category | flops | bytes accessed | tf_op | source)
XLA Modules:
  0.0 622.4 jit_solution(2819054057416116378)
XLA Ops:
  7.2 0.0 copy-start
  7.2 0.0 copy-start.5
  7.2 0.0 reduce-scatter.2.cloned.1.call-start
  7.3 0.0 copy-start.7
  7.3 0.0 copy-start.3
  7.3 0.6 copy-done.7
  7.9 0.6 dynamic_slice.15
  9.2 0.0 copy-done.5
  9.2 0.0 copy-start.2
  9.2 0.0 copy-start.6
  9.2 0.0 copy-done.3
  9.2 0.7 copy-done.2
  9.9 0.0 copy-done.6
  9.9 0.3 fusion.17
  10.2 0.0 copy-done
  10.2 0.3 broadcast_select_fusion
  10.5 129.4 %all-reduce.1 = (f32[32,128]{1,0:T(8,128)S(1)}, f32[64,128]{1,0:T(8,128)S(1)}) all-reduce(f32[32,128]{1,0:T(8,128)S(1)} %broadcast_select_fusion.1, f32[64,128]{1,0:T(8,128)S(1)} %get-tuple-element.153), channel_id=1, replica_groups=mesh['row'=16,'col'=32] {'col'}, use_global_device_ids=true, to_apply=%region_1.2 | all-reduce | flops 12288 | bytes 98304 | tf_op jit(solution)/shard_map/psum | solution.py:11
  139.9 0.0 copy-start.4
  139.9 0.7 copy-done.4
  140.6 32.7 %all_gather.7 = f32[32,2048]{1,0:T(8,128)S(1)} all-gather(f32[32,128]{1,0:T(8,128)S(1)} %copy-done.4), channel_id=1, replica_groups=mesh['row'=16,'col'=32] {'row'}, dimensions={1}, use_global_device_ids=true | all-gather | bytes 278528 | tf_op jit(solution)/shard_map/all_gather | solution.py:74
  173.3 0.2 reshape.23
  173.5 26.2 %all_gather.6 = f32[64,2048]{1,0:T(8,128)S(1)} all-gather(f32[64,128]{1,0:T(8,128)S(1)} %get-tuple-element.154), channel_id=1, replica_groups=mesh['row'=16,'col'=32] {'row'}, dimensions={1}, use_global_device_ids=true | all-gather | bytes 557056 | tf_op jit(solution)/shard_map/all_gather | solution.py:73
  199.7 7.0 %while.15 = (s32[]{:T(128)}, f32[64,128]{1,0:T(8,128)S(1)}, f32[2,64,1024]{2,1,0:T(8,128)S(1)}, f32[2,64,1024]{2,1,0:T(8,128)S(1)}, f32[2,32,1024]{2,0,1:T(2,128...) while((s32[]{:T(128)}, f32[64,128]{1,0:T(8,128)S(1)}, ...), condition=%wide.region_7.8_spmd.clone, body=%wide.region_3.0_spmd.clone.sunk | while | flops 353531776 | bytes 4523659 | solution.py:42
  199.8 0.1 constant_dynamic-slice_fusion.2
  199.9 1.0 fusion.56
  201.0 1.1 fusion.57
  202.1 0.5 fusion.58
  202.5 0.7 fusion.59
  203.3 0.1 constant_dynamic-slice_fusion.2
  203.4 1.0 fusion.56
  204.5 1.1 fusion.57
  205.6 0.5 fusion.58
  206.0 0.7 fusion.59
  206.7 0.8 copy.18
  207.6 0.0 reduce-scatter.2.cloned.1.call-update
  207.6 0.0 all-reduce.4.cloned.1.call-start
  207.7 142.1 %psum.44 = f32[64,128]{1,0:T(8,128)S(1)} all-reduce(f32[64,128]{1,0:T(8,128)S(1)} %get-tuple-element.94), channel_id=1, replica_groups=mesh['row'=16,'col'=32] {'col'}, use_global_device_ids=true, to_apply=%region_9.10 | all-reduce | flops 8192 | bytes 65536 | tf_op jit(solution)/shard_map/psum | solution.py:61
  349.8 0.0 reduce-scatter.2.cloned.1.call-done
  349.8 1.6 fusion.18
  351.4 0.0 copy-start.1
  351.4 0.0 all-reduce.4.cloned.1.call-update
  351.4 0.7 copy-done.1
  352.2 0.3 fusion.22
  352.5 0.2 convolution_bitcast_fusion.4
  352.7 101.5 %all-reduce = (f32[20,256]{1,0:T(8,128)}, f32[256]{0:T(256)}) all-reduce(f32[20,256]{1,0:T(8,128)S(1)} %convolution_bitcast_fusion.4, f32[256]{0:T(256)S(1)} %get-tuple-element.155), channel_id=1, replica_groups=mesh['row'=16,'col'=32] {'row','col'}, use_global_device_ids=true, to_apply=%region_10.11 | all-reduce | flops 5376 | bytes 43008 | tf_op jit(solution)/shard_map/psum | solution.py:80
  454.2 159.8 %all-reduce.4.cloned.1.call-done = f32[256,64]{0,1:T(8,128)} async-done(((f32[256,64]{0,1:T(8,128)}), f32[256,64]{0,1:T(8,128)}) %all-reduce.4.cloned.1.call-update) | async-done | bytes 65552 | tf_op jit(solution)/shard_map/psum | solution.py:80
  614.1 1.5 copy.38
  (7 shorter events, 0.1 us)
Async XLA Ops:
  7.2 3.0 copy-start
  7.2 2.0 copy-start.5
  7.2 342.6 %reduce-scatter.2.cloned.1.call-start = ((), (), s32[]{:S(2)}) async-start(), calls=%async_computation.1 | async-start | bytes 557056 | tf_op jit(solution)/shard_map/reduce_scatter | solution.py:76
  7.3 0.7 copy-start.7
  7.3 1.9 copy-start.3
  9.2 0.7 copy-start.2
  9.2 0.7 copy-start.6
  139.9 0.7 copy-start.4
  207.6 406.5 %all-reduce.4.cloned.1.call-start = ((), (), s32[]{:S(2)}) async-start(), calls=%async_computation.2 | async-start | bytes 131072 | tf_op jit(solution)/shard_map/psum | solution.py:80
  351.4 0.8 copy-start.1
Sparse Core Ops, SparseCore 0:
  207.7 75.7 reduce-scatter.1
  351.6 262.4 all-reduce.3
where the time goes:
time: 623 us; the launch traced here: 622 us
  blocking collectives  432 us (69%)
  waiting for transfers between devices  160 us (26%)
  between operations  14.8 us (2%)
  matrix products  9.29 us (1%)
    psum x1, waiting for transfers between devices, per_device(): lax.psum((terms[0], terms[1], terms[2]), ('row', 'col'))  160 us
    psum x1, blocking collectives, window_total(): return lax.psum(partial_grad, 'col')  142 us
    psum x1, blocking collectives, spread(): return lax.psum(kept, axis)  129 us
    psum x1, blocking collectives, per_device(): lax.psum((terms[0], terms[1], terms[2]), ('row', 'col'))  102 us
    all_gather x1, blocking collectives, per_device(): lax.all_gather(probes, 'row', axis=1, tiled=True)  32.7 us
    all_gather x1, blocking collectives, per_device(): lax.all_gather(features, 'row', axis=1, tiled=True)  26.2 us
  transfers between devices with their start and end apart: 2, of which 1 were waited for; matrix products, arithmetic and copies ran while one was open for 0% of the time, Pallas kernels for 0%

commit v1 on v0

--- a/solution.py
+++ b/solution.py
@@ -4,6 +4,16 @@
 from jax.sharding import PartitionSpec as P
 
 HIGHEST = lax.Precision.HIGHEST
+
+
+def lead_frame_on_mesh(local_array):
+    work_now = jax.lax.all_to_all(
+        jnp.stack([local_array for _ in range(jax.lax.axis_size("row"))]),
+        concat_axis=0,
+        split_axis=0,
+        axis_name="row",
+    )
+    return jnp.concatenate(work_now, 1)
 
 
 def spread(value, axis, source):
@@ -71,7 +81,7 @@
         window[0],
         window[1],
         lax.all_gather(features, "row", axis=1, tiled=True),
-        lax.all_gather(probes, "row", axis=1, tiled=True),
+        lead_frame_on_mesh(probes),
     )
     col_grad = lax.psum_scatter(col_part, "row", scatter_dimension=1, tiled=True)
     summed = window_total(win_part)

time: 623 us -> 595 us (0.955)
  blocking collectives: 432 us -> 388 us
  starting transfers between devices: 0.08 us -> 12.1 us
    all_gather x1 -> x0, blocking collectives: 32.7 us -> none  [per_device(): lax.all_gather(probes, 'row', axis=1, tiled=True)]
    psum x1, blocking collectives: 142 us -> 129 us  [window_total(): return lax.psum(partial_grad, 'col')]
    all_to_all x0 -> x1, starting transfers between devices: none -> 12 us  [lead_frame_on_mesh(): jax.lax.all_to_all(jnp.stack([local_array for _ in range(jax.lax.axis_siz...]
  transfers between devices with their start and end apart: 2 -> 3, of which waited for: 1 -> 1; matrix products, arithmetic and copies ran while one was open for 0% -> 0% of each run, Pallas kernels for 0% -> 0%
where the time goes in v1:
time: 595 us; the launch traced here: 594 us
  blocking collectives  388 us (65%)
  waiting for transfers between devices  162 us (27%)
  between operations  14.8 us (2%)
  starting transfers between devices  12.1 us (2%)
  matrix products  9.29 us (2%)
  local copies, waits for them, and re-layouts  6.99 us (1%)
    psum x1, waiting for transfers between devices, per_device(): lax.psum((terms[0], terms[1], terms[2]), ('row', 'col'))  162 us
    psum x1, blocking collectives, spread(): return lax.psum(kept, axis)  131 us
    psum x1, blocking collectives, window_total(): return lax.psum(partial_grad, 'col')  129 us
    psum x1, blocking collectives, per_device(): lax.psum((terms[0], terms[1], terms[2]), ('row', 'col'))  99.2 us
    all_gather x1, blocking collectives, per_device(): lax.all_gather(features, 'row', axis=1, tiled=True)  29.5 us
    all_to_all x1, starting transfers between devices, lead_frame_on_mesh(): jax.lax.all_to_all(jnp.stack([local_array for _ in range(jax.lax.axis_siz...  12 us
  transfers between devices with their start and end apart: 3, of which 1 were waited for; matrix products, arithmetic and copies ran while one was open for 0% of the time, Pallas kernels for 0%

profile of v1, /device:TPU:1, one launch (start us, length us, event | category | flops | bytes accessed | tf_op | source)
XLA Modules:
  0.0 593.9 jit_solution(7067267734903227665)
XLA Ops:
  7.2 0.0 copy-start
  7.2 1.5 stack.2
  8.6 0.0 copy-start.3
  8.6 12.0 %all-to-all-start = ((f32[16,32,128]{2,1,0:T(8,128)}), f32[16,32,128]{2,1,0:T(8,128)S(1)}, u32[]{:S(2)}, u32[]{:S(2)}) async-start(f32[16,32,128]{2,1,0:T(8,128)} %stack.2), calls=%async_computation | async-start | bytes 524288 | tf_op jit(solution)/shard_map/all_to_all | solution.py:10
  20.7 0.0 reduce-scatter.2.cloned.1.call-start
  20.7 0.0 copy-start.2
  20.8 0.0 copy-start.6
  20.8 0.6 copy-done.6
  21.4 0.6 dynamic_slice.15
  22.0 0.0 copy-start.5
  22.7 0.0 copy-done.3
  22.7 0.0 copy-done.2
  22.7 0.0 copy-done.5
  22.7 0.3 fusion.17
  23.0 0.0 copy-done
  23.0 0.3 broadcast_select_fusion
  23.3 29.5 %all_gather.3 = f32[64,2048]{1,0:T(8,128)S(1)} all-gather(f32[64,128]{1,0:T(8,128)S(1)} %get-tuple-element.162), channel_id=1, replica_groups=mesh['row'=16,'col'=32] {'row'}, dimensions={1}, use_global_device_ids=true | all-gather | bytes 557056 | tf_op jit(solution)/shard_map/all_gather | solution.py:83
  52.8 0.0 copy-start.4
  52.8 0.7 copy-done.4
  53.5 131.2 %all-reduce.1 = (f32[32,128]{1,0:T(8,128)S(1)}, f32[64,128]{1,0:T(8,128)S(1)}) all-reduce(f32[32,128]{1,0:T(8,128)S(1)} %broadcast_select_fusion.1, f32[64,128]{1,0:T(8,128)S(1)} %get-tuple-element.161), channel_id=1, replica_groups=mesh['row'=16,'col'=32] {'col'}, use_global_device_ids=true, to_apply=%region_1.2 | all-reduce | flops 12288 | bytes 98304 | tf_op jit(solution)/shard_map/psum | solution.py:21
  184.7 0.0 all-to-all-done
  184.7 0.2 copy.17
  184.9 0.1 reshape_reshape.3
  185.1 7.0 %while.15 = (s32[]{:T(128)}, f32[64,128]{1,0:T(8,128)S(1)}, f32[2,64,1024]{2,1,0:T(8,128)S(1)}, f32[2,64,1024]{2,1,0:T(8,128)S(1)}, f32[2,32,1024]{2,0,1:T(2,128...) while((s32[]{:T(128)}, f32[64,128]{1,0:T(8,128)S(1)}, ...), condition=%wide.region_7.8_spmd.clone, body=%wide.region_3.0_spmd.clone.sunk | while | flops 353531776 | bytes 4523659 | solution.py:52
  185.1 0.1 constant_dynamic-slice_fusion.2
  185.2 1.0 fusion.56
  186.3 1.1 fusion.57
  187.4 0.5 fusion.58
  187.8 0.7 fusion.59
  188.6 0.1 constant_dynamic-slice_fusion.2
  188.7 1.0 fusion.56
  189.8 1.1 fusion.57
  190.9 0.5 fusion.58
  191.3 0.7 fusion.59
  192.1 0.8 copy.22
  192.9 0.0 reduce-scatter.2.cloned.1.call-update
  192.9 0.0 all-reduce.4.cloned.1.call-start
  193.0 128.5 %psum.44 = f32[64,128]{1,0:T(8,128)S(1)} all-reduce(f32[64,128]{1,0:T(8,128)S(1)} %get-tuple-element.94), channel_id=1, replica_groups=mesh['row'=16,'col'=32] {'col'}, use_global_device_ids=true, to_apply=%region_9.10 | all-reduce | flops 8192 | bytes 65536 | tf_op jit(solution)/shard_map/psum | solution.py:71
  321.5 0.0 reduce-scatter.2.cloned.1.call-done
  321.5 1.6 fusion.18
  323.1 0.0 copy-start.1
  323.1 0.0 all-reduce.4.cloned.1.call-update
  323.1 0.7 copy-done.1
  323.9 0.3 fusion.22
  324.2 0.2 convolution_bitcast_fusion.4
  324.4 99.2 %all-reduce = (f32[20,256]{1,0:T(8,128)}, f32[256]{0:T(256)}) all-reduce(f32[20,256]{1,0:T(8,128)S(1)} %convolution_bitcast_fusion.4, f32[256]{0:T(256)S(1)} %get-tuple-element.163), channel_id=1, replica_groups=mesh['row'=16,'col'=32] {'row','col'}, use_global_device_ids=true, to_apply=%region_10.11 | all-reduce | flops 5376 | bytes 43008 | tf_op jit(solution)/shard_map/psum | solution.py:90
  423.6 162.0 %all-reduce.4.cloned.1.call-done = f32[256,64]{0,1:T(8,128)} async-done(((f32[256,64]{0,1:T(8,128)}), f32[256,64]{0,1:T(8,128)}) %all-reduce.4.cloned.1.call-update) | async-done | bytes 65552 | tf_op jit(solution)/shard_map/psum | solution.py:90
  585.6 1.5 copy.42
  (7 shorter events, 0.1 us)
Async XLA Ops:
  7.2 15.9 %copy-start = (f32[256,64]{0,1:T(8,128)S(1)}, f32[256,64]{0,1:T(8,128)}, u32[]{:S(2)}) copy-start(f32[256,64]{0,1:T(8,128)} %param.12) | copy-start | bytes 196612
  8.6 14.0 %copy-start.3 = (f32[20,256]{1,0:T(8,128)S(1)}, f32[20,256]{1,0:T(8,128)}, u32[]{:S(2)}) copy-start(f32[20,256]{1,0:T(8,128)} %param.10) | copy-start | bytes 61444
  8.6 176.1 %all-to-all-start = ((f32[16,32,128]{2,1,0:T(8,128)}), f32[16,32,128]{2,1,0:T(8,128)S(1)}, u32[]{:S(2)}, u32[]{:S(2)}) async-start(f32[16,32,128]{2,1,0:T(8,128)} %stack.2), calls=%async_computation | async-start | bytes 524288 | tf_op jit(solution)/shard_map/all_to_all | solution.py:10
  20.7 300.8 %reduce-scatter.2.cloned.1.call-start = ((), (), s32[]{:S(2)}) async-start(), calls=%async_computation.2 | async-start | bytes 557056 | tf_op jit(solution)/shard_map/reduce_scatter | solution.py:86
  20.7 1.9 copy-start.2
  20.8 0.7 copy-start.6
  22.0 0.7 copy-start.5
  52.8 0.7 copy-start.4
  192.9 392.7 %all-reduce.4.cloned.1.call-start = ((), (), s32[]{:S(2)}) async-start(), calls=%async_computation.3 | async-start | bytes 131072 | tf_op jit(solution)/shard_map/psum | solution.py:90
  323.1 0.8 copy-start.1
Sparse Core Ops, SparseCore 0:
  193.0 62.3 reduce-scatter.1
  323.2 262.2 all-reduce.3
